TPU v7x, 128 devices: a whole 4x4x4 slice. The times are simulated.
128 devices in a mesh: cell: 16 (over x, z_hi, core), tm: 8 (over y, z_lo).
Axes of the slice: x: 4, y: 4, z: 4 (z_hi: 2, z_lo: 2; z = z_hi * 2 + z_lo), core: 2. Of those that a mesh axis runs over, the one named last changes fastest.
Arguments:
- window: float32 [16384, 16384], P('cell', 'tm'), may hold values from -0.09375 to 0.09375
- range_test: float32 [16384, 256], P('tm'), may hold values from -0.046875 to 0.046875
- co_test: float32 [256, 16384], P(None, 'cell'), may hold values from -0.046875 to 0.046875
- core_left: float32 [512, 16384], P(None, 'cell'), may hold values from -0.046875 to 0.046875
- core_right: float32 [512, 16384], P(None, 'tm'), may hold values from -0.046875 to 0.046875
Outputs:
- range_basis: float32 [16384, 256], P('cell')
- co_basis: float32 [256, 16384], P(None, 'tm')
- core: float32 [256, 256], replicated
All inputs are finite; a program needn't handle non-finite values.
Results may differ from a plain program's by a relative error of at most 0.00023.
Values sent between devices are 32-bit elements; how exact they have to be, the bound alone decides.
A program may use at most 128 MiB of HBM per device.

v0:
```python
import math
import jax
import jax.numpy as jnp
from jax import lax
from jax.sharding import PartitionSpec as P


def inner_rows(left, right):
    return lax.dot_general(left, right, (((0,), (0,)), ((), ())), precision=lax.Precision.HIGHEST)


def inner_cols(left, right):
    return lax.dot_general(left, right, (((1,), (1,)), ((), ())), precision=lax.Precision.HIGHEST)


def product(left, right):
    return jnp.dot(left, right, precision=lax.Precision.HIGHEST, preferred_element_type=jnp.float32)


def per_device(window, range_test, co_test, core_left, core_right):
    rows_total = window.shape[0] * lax.axis_size("cell")
    cols_total = window.shape[1] * lax.axis_size("tm")
    range_term = product(window, range_test)
    co_term = product(co_test, window)
    left_window = product(core_left, window)
    core_term = inner_cols(left_window, core_right)
    sketch_z = lax.psum(core_term, ("cell", "tm"))
    range_full = lax.psum(range_term, "tm")
    co_full = lax.psum(co_term, "cell")
    gram_y = lax.psum(inner_rows(range_full, range_full) / rows_total, "cell")
    gram_w = lax.psum(inner_cols(co_full, co_full) / cols_total, "tm")
    lower_y = jnp.linalg.cholesky(gram_y)
    lower_w = jnp.linalg.cholesky(gram_w)
    range_basis = jax.scipy.linalg.solve_triangular(lower_y, range_full.T, lower=True).T
    co_basis = jax.scipy.linalg.solve_triangular(lower_w, co_full, lower=True)
    left_image = lax.psum(product(core_left, range_basis), "cell")
    right_image = lax.psum(inner_cols(core_right, co_basis), "tm")
    gram_left = inner_rows(left_image, left_image)
    gram_right = inner_rows(right_image, right_image)
    projected = inner_rows(left_image, sketch_z)
    left_solved = jax.scipy.linalg.cho_solve((jnp.linalg.cholesky(gram_left), True), projected)
    middle = product(left_solved, right_image)
    core = jax.scipy.linalg.cho_solve((jnp.linalg.cholesky(gram_right), True), middle.T).T
    core = core * math.sqrt(rows_total * cols_total)
    return (range_basis, co_basis, core)


def solution(mesh):
    return jax.shard_map(
        per_device,
        mesh=mesh,
        in_specs=(P("cell", "tm"), P("tm", None), P(None, "cell"), P(None, "cell"), P(None, "tm")),
        out_specs=(P("cell", None), P(None, "tm"), P()),
        check_vma=False,
    )
```

profile of v0, /device:TPU:0, one launch (start us, length us, event | category | flops | bytes accessed | tf_op | source)
XLA Modules:
  0.0 920.8 jit_solution(13198876106782574047)
XLA Ops:
  7.2 10.7 %fusion.50 = f32[1024,256]{1,0:T(8,128)} fusion(f32[1024,2048]{1,0:T(8,128)} %param.6, f32[2048,256]{1,0:T(8,128)} %param.7), kind=kOutput, calls=%fused_computation.123 | convolution fusion | flops 6442450944 | bytes 11534336 | tf_op jit(solution)/shard_map/dot_general | solution.py:17
  18.0 80.7 %all-reduce.9.cloned.1.call-done = f32[1024,256]{1,0:T(8,128)} async-done(((f32[1024,256]{1,0:T(8,128)}), f32[1024,256]{1,0:T(8,128)}) %all-reduce.9.cloned.1.call-update) | async-done | bytes 1048592 | tf_op jit(solution)/shard_map/psum | solution.py:28
  98.6 4.1 convolution_multiply_fusion.1
  102.8 10.7 %fusion.51 = f32[256,2048]{1,0:T(8,128)} fusion(f32[256,1024]{1,0:T(8,128)S(1)} %copy-done.12, f32[1024,2048]{1,0:T(8,128)} %param.6), kind=kOutput, calls=%fused_computation.124 | convolution fusion | flops 6442450944 | bytes 11534336 | tf_op jit(solution)/shard_map/dot_general | solution.py:17
  113.5 127.4 %all-reduce.11.cloned.1.call-done = f32[256,256]{0,1:T(8,128)} async-done(((f32[256,256]{0,1:T(8,128)}), f32[256,256]{0,1:T(8,128)}) %all-reduce.11.cloned.1.call-update) | async-done | bytes 262160 | tf_op jit(solution)/shard_map/psum | solution.py:30
  243.7 11.7 %cholesky.214 = f32[128,128]{1,0:T(8,128)S(1)} custom-call(f32[128,128]{1,0:T(8,128)S(1)} %cholesky.346), custom_call_target="Cholesky" | custom-call | tf_op jit(solution)/shard_map/jit(cholesky)/cholesky | solution.py:32
  255.5 9.8 %custom-call.37 = f32[1,128,128]{1,2,0:T(8,128)S(1)} custom-call(f32[1,128,128]{2,1,0:T(8,128)S(1)} %get-tuple-element.96), custom_call_target="InvertDiagBlocksLowerTriangular" | custom-call | tf_op jit(solution)/shard_map/jit(cholesky)/cholesky | solution.py:32
  267.4 11.7 %cholesky.231 = f32[128,128]{1,0:T(8,128)S(1)} custom-call(f32[128,128]{1,0:T(8,128)S(1)} %convolution_subtract_fusion.9), custom_call_target="Cholesky" | custom-call | tf_op jit(solution)/shard_map/jit(cholesky)/cholesky | solution.py:32
  282.3 4.1 while.4
  287.0 20.7 %custom-call.30 = f32[2,128,128]{1,2,0:T(8,128)S(1)} custom-call(f32[2,128,128]{2,1,0:T(8,128)} %copy-done.17), custom_call_target="InvertDiagBlocksLowerTriangular" | custom-call | tf_op jit(solution)/shard_map/jit(_solve_triangular)/triangular_solve | solution.py:34
  312.9 16.9 %fusion.54 = f32[512,2048]{1,0:T(8,128)S(1)} fusion(f32[512,1024]{1,0:T(8,128)S(1)} %copy-done, f32[1024,2048]{1,0:T(8,128)} %param.6), kind=kOutput, calls=%fused_computation.127 | convolution fusion | flops 12884901888 | bytes 14680064 | tf_op jit(solution)/shard_map/dot_general | solution.py:17
  329.8 7.9 fusion.55
  344.1 116.8 %all-reduce.19.cloned.1.call-done = (f32[256,2048]{1,0:T(8,128)}, f32[512,256]{0,1:T(8,128)}) async-done(((f32[256,2048]{1,0:T(8,128)}, f32[512,256]{0,1:T(8,128)}), (f32[256,2048]{1,0:T(8,128)}, f32[512,256]{0,1:T(8,128)})) %all-reduce.19.cloned.1.call-update) | async-done | bytes 2621456 | tf_op jit(solution)/shard_map/psum | solution.py:29
  462.9 11.7 %cholesky.316 = f32[128,128]{1,0:T(8,128)S(1)} custom-call(f32[128,128]{1,0:T(8,128)S(1)} %cholesky.355), custom_call_target="Cholesky" | custom-call | tf_op jit(solution)/shard_map/jit(cholesky)/cholesky | solution.py:41
  474.7 9.8 %custom-call.40 = f32[1,128,128]{1,2,0:T(8,128)S(1)} custom-call(f32[1,128,128]{2,1,0:T(8,128)S(1)} %get-tuple-element.88), custom_call_target="InvertDiagBlocksLowerTriangular" | custom-call | tf_op jit(solution)/shard_map/jit(cholesky)/cholesky | solution.py:41
  485.0 11.7 %cholesky.333 = f32[128,128]{1,0:T(8,128)S(1)} custom-call(f32[128,128]{1,0:T(8,128)S(1)} %convolution_subtract_fusion.6), custom_call_target="Cholesky" | custom-call | tf_op jit(solution)/shard_map/jit(cholesky)/cholesky | solution.py:41
  499.5 4.1 while.7
  503.6 19.7 %custom-call.33 = f32[2,128,128]{1,2,0:T(8,128)S(1)} custom-call(f32[2,128,128]{2,1,0:T(8,128)S(1)} %get-tuple-element.35), custom_call_target="InvertDiagBlocksLowerTriangular" | custom-call | tf_op jit(solution)/shard_map/jit(_cho_solve)/triangular_solve | solution.py:41
  523.3 4.8 convolution_multiply_fusion
  528.6 85.9 %all-reduce.17.cloned.1.call-done = f32[512,512]{1,0:T(8,128)} async-done(((f32[512,512]{1,0:T(8,128)}), f32[512,512]{1,0:T(8,128)}) %all-reduce.17.cloned.1.call-update) | async-done | bytes 1048592 | tf_op jit(solution)/shard_map/psum | solution.py:27
  618.1 73.0 %all-reduce.13.cloned.1.call-done = f32[256,256]{0,1:T(8,128)} async-done(((f32[256,256]{0,1:T(8,128)}), f32[256,256]{0,1:T(8,128)}) %all-reduce.13.cloned.1.call-update) | async-done | bytes 262160 | tf_op jit(solution)/shard_map/psum | solution.py:31
  693.2 11.7 %cholesky.248 = f32[128,128]{1,0:T(8,128)S(1)} custom-call(f32[128,128]{1,0:T(8,128)S(1)} %cholesky.349), custom_call_target="Cholesky" | custom-call | tf_op jit(solution)/shard_map/jit(cholesky)/cholesky | solution.py:33
  705.0 9.8 %custom-call.38 = f32[1,128,128]{1,2,0:T(8,128)S(1)} custom-call(f32[1,128,128]{2,1,0:T(8,128)S(1)} %get-tuple-element.92), custom_call_target="InvertDiagBlocksLowerTriangular" | custom-call | tf_op jit(solution)/shard_map/jit(cholesky)/cholesky | solution.py:33
  716.9 11.9 %cholesky.265 = f32[128,128]{1,0:T(8,128)S(1)} custom-call(f32[128,128]{1,0:T(8,128)S(1)} %convolution_subtract_fusion.8), custom_call_target="Cholesky" | custom-call | tf_op jit(solution)/shard_map/jit(cholesky)/cholesky | solution.py:33
  735.5 19.7 %custom-call.31 = f32[2,128,128]{1,2,0:T(8,128)S(1)} custom-call(f32[2,128,128]{2,1,0:T(8,128)S(1)} %get-tuple-element.19), custom_call_target="InvertDiagBlocksLowerTriangular" | custom-call | tf_op jit(solution)/shard_map/jit(_solve_triangular)/triangular_solve | solution.py:35
  762.6 4.5 convolution_bitcast_fusion.1
  768.3 73.2 %all-reduce.15.cloned.1.call-done = f32[512,256]{0,1:T(8,128)} async-done(((f32[512,256]{0,1:T(8,128)}), f32[512,256]{0,1:T(8,128)}) %all-reduce.15.cloned.1.call-update) | async-done | bytes 524304 | tf_op jit(solution)/shard_map/psum | solution.py:37
  845.9 11.9 %cholesky.282 = f32[128,128]{1,0:T(8,128)S(1)} custom-call(f32[128,128]{1,0:T(8,128)S(1)} %cholesky.352), custom_call_target="Cholesky" | custom-call | tf_op jit(solution)/shard_map/jit(cholesky)/cholesky | solution.py:43
  857.8 9.8 %custom-call.39 = f32[1,128,128]{1,2,0:T(8,128)S(1)} custom-call(f32[1,128,128]{2,1,0:T(8,128)S(1)} %get-tuple-element.84), custom_call_target="InvertDiagBlocksLowerTriangular" | custom-call | tf_op jit(solution)/shard_map/jit(cholesky)/cholesky | solution.py:43
  869.8 11.7 %cholesky.299 = f32[128,128]{1,0:T(8,128)S(1)} custom-call(f32[128,128]{1,0:T(8,128)S(1)} %convolution_subtract_fusion.7), custom_call_target="Cholesky" | custom-call | tf_op jit(solution)/shard_map/jit(cholesky)/cholesky | solution.py:43
  885.2 4.1 while.6
  890.0 20.5 %custom-call.32 = f32[2,128,128]{1,2,0:T(8,128)S(1)} custom-call(f32[2,128,128]{2,1,0:T(8,128)} %copy-done.16), custom_call_target="InvertDiagBlocksLowerTriangular" | custom-call | tf_op jit(solution)/shard_map/jit(_cho_solve)/triangular_solve | solution.py:43
  (150 shorter events, 74.1 us)
Async XLA Ops:
  7.2 302.9 %copy-start = (f32[512,1024]{1,0:T(8,128)S(1)}, f32[512,1024]{1,0:T(8,128)}, u32[]{:S(2)}) copy-start(f32[512,1024]{1,0:T(8,128)} %param.9) | copy-start | bytes 6291460
  7.2 91.5 %all-reduce.9.cloned.1.call-start = ((), (), s32[]{:S(2)}) async-start(), calls=%async_computation | async-start | bytes 2097152 | tf_op jit(solution)/shard_map/psum | solution.py:28
  17.9 84.9 %copy-start.12 = (f32[256,1024]{1,0:T(8,128)S(1)}, f32[256,1024]{1,0:T(8,128)}, u32[]{:S(2)}) copy-start(f32[256,1024]{1,0:T(8,128)} %param.8) | copy-start | bytes 3145732
  17.9 223.0 %all-reduce.11.cloned.1.call-start = ((), (), s32[]{:S(2)}) async-start(), calls=%async_computation.1 | async-start | bytes 524288 | tf_op jit(solution)/shard_map/psum | solution.py:30
  102.7 358.2 %all-reduce.19.cloned.1.call-start = ((), (), s32[]{:S(2)}) async-start(), calls=%async_computation.5 | async-start | bytes 5242880 | tf_op jit(solution)/shard_map/psum | solution.py:29
  113.5 194.2 %copy-start.4 = (f32[1024,256]{1,0:T(8,128)S(1)}, f32[1024,256]{1,0:T(8,128)}, u32[]{:S(2)}) copy-start(f32[1024,256]{1,0:T(8,128)} %all-reduce.9.cloned.1.call-done) | copy-start | bytes 3145732
  243.0 0.7 copy-start.13
  279.2 2.0 copy-start.10
  286.4 0.7 copy-start.17
  308.4 1.7 copy-start.5
  312.8 301.7 %all-reduce.17.cloned.1.call-start = ((), (), s32[]{:S(2)}) async-start(), calls=%async_computation.4 | async-start | bytes 2097152 | tf_op jit(solution)/shard_map/psum | solution.py:27
  312.9 16.9 %copy-start.2 = (f32[512,2048]{1,0:T(8,128)S(1)}, f32[512,2048]{1,0:T(8,128)}, u32[]{:S(2)}) copy-start(f32[512,2048]{1,0:T(8,128)} %param.10) | copy-start | bytes 12582916
  329.8 10.7 %copy-start.6 = (f32[128,1024]{1,0:T(8,128)S(1)}, f32[128,1024]{1,0:T(8,128)}, u32[]{:S(2)}) copy-start(f32[128,1024]{1,0:T(8,128)} %copy-done.5) | copy-start | bytes 1572868
  337.7 353.3 %all-reduce.13.cloned.1.call-start = ((), (), s32[]{:S(2)}) async-start(), calls=%async_computation.2 | async-start | bytes 524288 | tf_op jit(solution)/shard_map/psum | solution.py:31
  523.3 91.3 %copy-start.9 = (f32[512,256]{0,1:T(8,128)S(1)}, f32[512,256]{0,1:T(8,128)}, u32[]{:S(2)}) copy-start(f32[512,256]{0,1:T(8,128)} %get-tuple-element.72) | copy-start | bytes 1572868
  528.2 313.4 %all-reduce.15.cloned.1.call-start = ((), (), s32[]{:S(2)}) async-start(), calls=%async_computation.3 | async-start | bytes 1048576 | tf_op jit(solution)/shard_map/psum | solution.py:37
  693.2 11.7 %copy-start.14 = (f32[256,256]{1,0:T(8,128)}, f32[256,256]{1,0:T(8,128)S(1)}, u32[]{:S(2)}) copy-start(f32[256,256]{1,0:T(8,128)S(1)} %fusion.14) | copy-start | bytes 786436
  755.2 2.4 copy-start.1
  759.7 2.9 copy-start.3
  759.9 1.3 copy-start.7
  843.3 67.1 %copy-start.8 = (f32[512,256]{0,1:T(8,128)S(1)}, f32[512,256]{0,1:T(8,128)}, u32[]{:S(2)}) copy-start(f32[512,256]{0,1:T(8,128)} %all-reduce.15.cloned.1.call-done) | copy-start | bytes 1572868
  845.2 0.7 copy-start.15
  882.3 1.9 copy-start.11
  889.3 0.7 copy-start.16
Sparse Core Ops, SparseCore 0:
  18.1 80.5 all-reduce.8
  102.8 138.0 all-reduce.10
  313.0 147.9 all-reduce.18
  465.6 148.9 all-reduce.16
  617.4 73.6 all-reduce.12
  767.3 74.1 all-reduce.14
where the time goes:
time: 929 us; the launch traced here: 921 us
  waiting for transfers between devices  557 us (60%)
  other arithmetic  225 us (24%)
  matrix products  86.6 us (9%)
  local copies, waits for them, and re-layouts  28.3 us (3%)
  between operations  20.2 us (2%)
    psum x1, waiting for transfers between devices, per_device(): gram_y = lax.psum(inner_rows(range_full, range_full) / rows_total, 'cell')  127 us
    psum x1, waiting for transfers between devices, per_device(): co_full = lax.psum(co_term, 'cell')  117 us
    psum x1, waiting for transfers between devices, per_device(): sketch_z = lax.psum(core_term, ('cell', 'tm'))  85.9 us
    psum x1, waiting for transfers between devices, per_device(): range_full = lax.psum(range_term, 'tm')  80.7 us
    psum x1, waiting for transfers between devices, per_device(): right_image = lax.psum(inner_cols(core_right, co_basis), 'tm')  73.2 us
    psum x1, waiting for transfers between devices, per_device(): gram_w = lax.psum(inner_cols(co_full, co_full) / cols_total, 'tm')  73 us
    dot_general x5, matrix products, product(): jnp.dot(left, right, precision=lax.Precision.HIGHEST, preferred_element_t...  41.6 us
    another operation x7, other arithmetic, per_device(): jnp.linalg.cholesky(gram_right)  34.8 us
  transfers between devices with their start and end apart: 6, of which 6 were waited for; matrix products, arithmetic and copies ran while one was open for 12% of the time, Pallas kernels for 0%

commit v1 on v0

--- a/solution.py
+++ b/solution.py
@@ -24,7 +24,8 @@
     co_term = product(co_test, window)
     left_window = product(core_left, window)
     core_term = inner_cols(left_window, core_right)
-    sketch_z = lax.psum(core_term, ("cell", "tm"))
+    partial = lax.psum(core_term, "tm")
+    sketch_z = lax.psum(partial, "cell")
     range_full = lax.psum(range_term, "tm")
     co_full = lax.psum(co_term, "cell")
     gram_y = lax.psum(inner_rows(range_full, range_full) / rows_total, "cell")

time: 929 us -> 832 us (0.90)
  waiting for transfers between devices: 557 us -> 467 us
    psum x1 -> x0, waiting for transfers between devices: 85.9 us -> none  [per_device(): sketch_z = lax.psum(core_term, ('cell', 'tm'))]
    psum x1, waiting for transfers between devices: 73 us -> 10.3 us  [per_device(): gram_w = lax.psum(inner_cols(co_full, co_full) / cols_total, 'tm')]
    psum x1, waiting for transfers between devices: 117 us -> 148 us  [per_device(): co_full = lax.psum(co_term, 'cell')]
    psum x1, waiting for transfers between devices: 80.7 us -> 107 us  [per_device(): range_full = lax.psum(range_term, 'tm')]
  transfers between devices with their start and end apart: 6 -> 5, of which waited for: 6 -> 5; matrix products, arithmetic and copies ran while one was open for 12% -> 10% of each run, Pallas kernels for 0% -> 0%
where the time goes in v1:
time: 832 us; the launch traced here: 826 us
  waiting for transfers between devices  467 us (56%)
  other arithmetic  226 us (27%)
  matrix products  82.3 us (10%)
  local copies, waits for them, and re-layouts  30.5 us (4%)
  between operations  19.7 us (2%)
    psum x1, waiting for transfers between devices, per_device(): co_full = lax.psum(co_term, 'cell')  148 us
    psum x1, waiting for transfers between devices, per_device(): gram_y = lax.psum(inner_rows(range_full, range_full) / rows_total, 'cell')  129 us
    psum x1, waiting for transfers between devices, per_device(): range_full = lax.psum(range_term, 'tm')  107 us
    psum x1, waiting for transfers between devices, per_device(): right_image = lax.psum(inner_cols(core_right, co_basis), 'tm')  73 us
    dot_general x5, matrix products, product(): jnp.dot(left, right, precision=lax.Precision.HIGHEST, preferred_element_t...  38.4 us
    another operation x7, other arithmetic, per_device(): jnp.linalg.cholesky(gram_right)  34.8 us
    another operation x7, other arithmetic, per_device(): lower_w = jnp.linalg.cholesky(gram_w)  34.7 us
    another operation x7, other arithmetic, per_device(): jnp.linalg.cholesky(gram_left)  34.6 us
  transfers between devices with their start and end apart: 5, of which 5 were waited for; matrix products, arithmetic and copies ran while one was open for 10% of the time, Pallas kernels for 0%

profile of v1, /device:TPU:0, one launch (start us, length us, event | category | flops | bytes accessed | tf_op | source)
XLA Modules:
  0.0 825.9 jit_solution(2092319959878946442)
XLA Ops:
  8.8 16.6 %fusion.54 = f32[512,2048]{1,0:T(8,128)S(1)} fusion(f32[512,1024]{1,0:T(8,128)S(1)} %copy-done, f32[1024,2048]{1,0:T(8,128)} %param.6), kind=kOutput, calls=%fused_computation.127 | convolution fusion | flops 12884901888 | bytes 14680064 | tf_op jit(solution)/shard_map/dot_general | solution.py:17
  25.4 7.6 fusion.50
  33.1 8.1 fusion.55
  41.2 106.8 %all-reduce.17.cloned.1.call-done = (f32[1024,256]{1,0:T(8,128)}, f32[512,512]{1,0:T(8,128)}) async-done(((f32[1024,256]{1,0:T(8,128)}, f32[512,512]{1,0:T(8,128)}), (f32[1024,256]{1,0:T(8,128)}, f32[512,512]{1,0:T(8,128)})) %all-reduce.17.cloned.1.call-update) | async-done | bytes 2097168 | tf_op jit(solution)/shard_map/psum | solution.py:29
  148.0 4.1 convolution_multiply_fusion.1
  152.2 10.7 %fusion.51 = f32[256,2048]{1,0:T(8,128)} fusion(f32[256,1024]{1,0:T(8,128)S(1)} %copy-done.14, f32[1024,2048]{1,0:T(8,128)} %param.6), kind=kOutput, calls=%fused_computation.124 | convolution fusion | flops 6442450944 | bytes 11534336 | tf_op jit(solution)/shard_map/dot_general | solution.py:17
  162.9 129.4 %all-reduce.9.cloned.1.call-done = f32[256,256]{0,1:T(8,128)} async-done(((f32[256,256]{0,1:T(8,128)}), f32[256,256]{0,1:T(8,128)}) %all-reduce.9.cloned.1.call-update) | async-done | bytes 262160 | tf_op jit(solution)/shard_map/psum | solution.py:31
  295.1 11.7 %cholesky.214 = f32[128,128]{1,0:T(8,128)S(1)} custom-call(f32[128,128]{1,0:T(8,128)S(1)} %cholesky.346), custom_call_target="Cholesky" | custom-call | tf_op jit(solution)/shard_map/jit(cholesky)/cholesky | solution.py:33
  306.8 9.8 %custom-call.37 = f32[1,128,128]{1,2,0:T(8,128)S(1)} custom-call(f32[1,128,128]{2,1,0:T(8,128)S(1)} %get-tuple-element.99), custom_call_target="InvertDiagBlocksLowerTriangular" | custom-call | tf_op jit(solution)/shard_map/jit(cholesky)/cholesky | solution.py:33
  318.8 11.7 %cholesky.231 = f32[128,128]{1,0:T(8,128)S(1)} custom-call(f32[128,128]{1,0:T(8,128)S(1)} %convolution_subtract_fusion.9), custom_call_target="Cholesky" | custom-call | tf_op jit(solution)/shard_map/jit(cholesky)/cholesky | solution.py:33
  333.6 4.1 while.4
  338.4 20.9 %custom-call.30 = f32[2,128,128]{1,2,0:T(8,128)S(1)} custom-call(f32[2,128,128]{2,1,0:T(8,128)} %copy-done.19), custom_call_target="InvertDiagBlocksLowerTriangular" | custom-call | tf_op jit(solution)/shard_map/jit(_solve_triangular)/triangular_solve | solution.py:35
  369.0 147.7 %all-reduce.15.cloned.1.call-done = (f32[256,2048]{1,0:T(8,128)}, f32[512,256]{0,1:T(8,128)}, f32[512,512]{1,0:T(8,128)}) async-done(((f32[256,2048]{1,0:T(8,128)}, f32[512,256]{0,1:T(8,128)}, f32[512,512]{1,0:T(8,128)}), (f32[256,2048]{1,0:T(8,128)}, f32[512,256]{0,1:T(8,128)}, f32[512,512]{1,0:T(8,128)})) %all-reduce.15.cloned.1.call-update) | async-done | bytes 3670032 | tf_op jit(solution)/shard_map/psum | solution.py:30
  516.7 4.8 convolution_multiply_fusion
  522.6 11.7 %cholesky.316 = f32[128,128]{1,0:T(8,128)S(1)} custom-call(f32[128,128]{1,0:T(8,128)S(1)} %cholesky.355), custom_call_target="Cholesky" | custom-call | tf_op jit(solution)/shard_map/jit(cholesky)/cholesky | solution.py:42
  534.4 9.8 %custom-call.40 = f32[1,128,128]{1,2,0:T(8,128)S(1)} custom-call(f32[1,128,128]{2,1,0:T(8,128)S(1)} %get-tuple-element.91), custom_call_target="InvertDiagBlocksLowerTriangular" | custom-call | tf_op jit(solution)/shard_map/jit(cholesky)/cholesky | solution.py:42
  544.7 11.7 %cholesky.333 = f32[128,128]{1,0:T(8,128)S(1)} custom-call(f32[128,128]{1,0:T(8,128)S(1)} %convolution_subtract_fusion.6), custom_call_target="Cholesky" | custom-call | tf_op jit(solution)/shard_map/jit(cholesky)/cholesky | solution.py:42
  559.0 3.8 while.7
  562.8 20.1 %custom-call.33 = f32[2,128,128]{1,2,0:T(8,128)S(1)} custom-call(f32[2,128,128]{2,1,0:T(8,128)S(1)} %get-tuple-element.35), custom_call_target="InvertDiagBlocksLowerTriangular" | custom-call | tf_op jit(solution)/shard_map/jit(_cho_solve)/triangular_solve | solution.py:42
  586.4 10.3 %all-reduce.11.cloned.1.call-done = f32[256,256]{0,1:T(8,128)} async-done(((f32[256,256]{0,1:T(8,128)}), f32[256,256]{0,1:T(8,128)}) %all-reduce.11.cloned.1.call-update) | async-done | bytes 262160 | tf_op jit(solution)/shard_map/psum | solution.py:32
  598.8 11.7 %cholesky.248 = f32[128,128]{1,0:T(8,128)S(1)} custom-call(f32[128,128]{1,0:T(8,128)S(1)} %cholesky.349), custom_call_target="Cholesky" | custom-call | tf_op jit(solution)/shard_map/jit(cholesky)/cholesky | solution.py:34
  610.6 9.8 %custom-call.38 = f32[1,128,128]{1,2,0:T(8,128)S(1)} custom-call(f32[1,128,128]{2,1,0:T(8,128)S(1)} %get-tuple-element.95), custom_call_target="InvertDiagBlocksLowerTriangular" | custom-call | tf_op jit(solution)/shard_map/jit(cholesky)/cholesky | solution.py:34
  622.5 11.7 %cholesky.265 = f32[128,128]{1,0:T(8,128)S(1)} custom-call(f32[128,128]{1,0:T(8,128)S(1)} %convolution_subtract_fusion.8), custom_call_target="Cholesky" | custom-call | tf_op jit(solution)/shard_map/jit(cholesky)/cholesky | solution.py:34
  637.1 4.0 while.5
  641.1 19.7 %custom-call.31 = f32[2,128,128]{1,2,0:T(8,128)S(1)} custom-call(f32[2,128,128]{2,1,0:T(8,128)S(1)} %get-tuple-element.19), custom_call_target="InvertDiagBlocksLowerTriangular" | custom-call | tf_op jit(solution)/shard_map/jit(_solve_triangular)/triangular_solve | solution.py:36
  668.2 4.5 convolution_bitcast_fusion.1
  673.9 73.0 %all-reduce.13.cloned.1.call-done = f32[512,256]{0,1:T(8,128)} async-done(((f32[512,256]{0,1:T(8,128)}), f32[512,256]{0,1:T(8,128)}) %all-reduce.13.cloned.1.call-update) | async-done | bytes 524304 | tf_op jit(solution)/shard_map/psum | solution.py:38
  751.3 11.9 %cholesky.282 = f32[128,128]{1,0:T(8,128)S(1)} custom-call(f32[128,128]{1,0:T(8,128)S(1)} %cholesky.352), custom_call_target="Cholesky" | custom-call | tf_op jit(solution)/shard_map/jit(cholesky)/cholesky | solution.py:44
  763.3 9.8 %custom-call.39 = f32[1,128,128]{1,2,0:T(8,128)S(1)} custom-call(f32[1,128,128]{2,1,0:T(8,128)S(1)} %get-tuple-element.87), custom_call_target="InvertDiagBlocksLowerTriangular" | custom-call | tf_op jit(solution)/shard_map/jit(cholesky)/cholesky | solution.py:44
  775.3 11.7 %cholesky.299 = f32[128,128]{1,0:T(8,128)S(1)} custom-call(f32[128,128]{1,0:T(8,128)S(1)} %convolution_subtract_fusion.7), custom_call_target="Cholesky" | custom-call | tf_op jit(solution)/shard_map/jit(cholesky)/cholesky | solution.py:44
  790.6 4.1 while.6
  795.4 20.5 %custom-call.32 = f32[2,128,128]{1,2,0:T(8,128)S(1)} custom-call(f32[2,128,128]{2,1,0:T(8,128)} %copy-done.18), custom_call_target="InvertDiagBlocksLowerTriangular" | custom-call | tf_op jit(solution)/shard_map/jit(_cho_solve)/triangular_solve | solution.py:44
  (151 shorter events, 68.2 us)
Async XLA Ops:
  7.2 1.6 copy-start
  7.2 140.8 %all-reduce.17.cloned.1.call-start = ((), (), s32[]{:S(2)}) async-start(), calls=%async_computation.4 | async-start | bytes 4194304 | tf_op jit(solution)/shard_map/psum | solution.py:29
  8.8 16.6 %copy-start.1 = (f32[1024,2048]{1,0:T(8,128)S(1)}, f32[1024,2048]{1,0:T(8,128)}, u32[]{:S(2)}) copy-start(f32[1024,2048]{1,0:T(8,128)} %param.6) | copy-start | bytes 25165828
  8.8 16.7 %copy-start.11 = (f32[2048,256]{1,0:T(8,128)S(1)}, f32[2048,256]{1,0:T(8,128)}, u32[]{:S(2)}) copy-start(f32[2048,256]{1,0:T(8,128)} %param.7) | copy-start | bytes 6291460
  25.4 7.6 copy-start.3
  41.1 111.0 %copy-start.14 = (f32[256,1024]{1,0:T(8,128)S(1)}, f32[256,1024]{1,0:T(8,128)}, u32[]{:S(2)}) copy-start(f32[256,1024]{1,0:T(8,128)} %param.8) | copy-start | bytes 3145732
  41.2 251.1 %all-reduce.9.cloned.1.call-start = ((), (), s32[]{:S(2)}) async-start(), calls=%async_computation | async-start | bytes 524288 | tf_op jit(solution)/shard_map/psum | solution.py:31
  152.1 364.6 %all-reduce.15.cloned.1.call-start = ((), (), s32[]{:S(2)}) async-start(), calls=%async_computation.3 | async-start | bytes 7340032 | tf_op jit(solution)/shard_map/psum | solution.py:30
  162.9 196.4 %copy-start.5 = (f32[1024,256]{1,0:T(8,128)S(1)}, f32[1024,256]{1,0:T(8,128)}, u32[]{:S(2)}) copy-start(f32[1024,256]{1,0:T(8,128)} %get-tuple-element.74) | copy-start | bytes 3145732
  294.4 0.7 copy-start.15
  330.6 2.0 copy-start.13
  337.7 0.7 copy-start.19
  359.9 4.4 copy-start.6
  364.4 1.0 copy-start.7
  364.4 232.3 %all-reduce.11.cloned.1.call-start = ((), (), s32[]{:S(2)}) async-start(), calls=%async_computation.1 | async-start | bytes 524288 | tf_op jit(solution)/shard_map/psum | solution.py:32
  516.7 5.1 copy-start.10
  521.6 225.4 %all-reduce.13.cloned.1.call-start = ((), (), s32[]{:S(2)}) async-start(), calls=%async_computation.2 | async-start | bytes 1048576 | tf_op jit(solution)/shard_map/psum | solution.py:38
  598.8 11.7 %copy-start.16 = (f32[256,256]{1,0:T(8,128)}, f32[256,256]{1,0:T(8,128)S(1)}, u32[]{:S(2)}) copy-start(f32[256,256]{1,0:T(8,128)S(1)} %fusion.14) | copy-start | bytes 786436
  660.8 2.4 copy-start.2
  665.3 2.9 copy-start.4
  665.5 1.3 copy-start.8
  748.8 67.1 %copy-start.9 = (f32[512,256]{0,1:T(8,128)S(1)}, f32[512,256]{0,1:T(8,128)}, u32[]{:S(2)}) copy-start(f32[512,256]{0,1:T(8,128)} %all-reduce.13.cloned.1.call-done) | copy-start | bytes 1572868
  750.6 0.7 copy-start.17
  787.0 2.6 copy-start.12
  794.8 0.7 copy-start.18
Sparse Core Ops, SparseCore 0:
  41.3 106.6 all-reduce.16
  152.2 140.0 all-reduce.8
  364.5 152.1 all-reduce.14
  521.7 74.9 all-reduce.10
  672.9 74.0 all-reduce.12
